TPU v7x, 32 devices: a whole 2x2x4 slice. The times are simulated.
32 devices in a mesh: gx: 4 (over z), gy: 8 (over y, x, core).
Axes of the slice: x: 2, y: 2, z: 4, core: 2. Of those that a mesh axis runs over, the one named last changes fastest.
Arguments:
- data: bfloat16 [128, 512, 1024], P(None, 'gx', 'gy')
- inv_scale: float32 [128], replicated, may hold values from 0.1 to 1
- start: float32 [128, 32], replicated, may hold values from -6 to 6
- rank: int32 [1], replicated, may hold values from 24 to 32
Outputs:
- core: bfloat16 [32, 512, 1024], P(None, 'gx', 'gy')
- factor: float32 [128, 32], replicated
Inputs may be any that keep to these rules, and one draw needn't show every extreme that they name: rank[0] is the number of leading columns of the factor that are kept.
All inputs are finite; a program needn't handle non-finite values.
Results may differ from a plain program's by a relative error of at most 0.0044.
Values sent between devices are 32-bit elements; how exact they have to be, the bound alone decides.
A program may use at most 64 MiB of HBM per device.

v0:
```python
import jax
import jax.numpy as jnp
from jax import lax
from jax.sharding import PartitionSpec as P

ITERS = 4


def body(data, inv_scale, start, rank):
    variables = data.shape[0]
    columns = start.shape[1]
    flat = data.reshape(variables, -1)
    local_gram = lax.dot_general(
        flat, flat, (((1,), (1,)), ((), ())), preferred_element_type=jnp.float32
    )
    gram = lax.psum(local_gram, ("gx", "gy"))
    weighted = inv_scale[:, None] * gram * inv_scale[None, :]
    basis = start
    for turn in range(ITERS):
        image = jnp.dot(weighted, basis, precision=lax.Precision.HIGHEST)
        inner = jnp.dot(image.T, image, precision=lax.Precision.HIGHEST)
        lower = jnp.linalg.cholesky(inner)
        basis = lax.linalg.triangular_solve(
            lower, image, left_side=False, lower=True, transpose_a=True
        )
    keep = (jnp.arange(columns, dtype=jnp.int32) < rank[0]).astype(jnp.float32)
    factor = basis * keep[None, :]
    scaled_factor = (inv_scale[:, None] * factor).astype(jnp.bfloat16)
    product = lax.dot_general(
        scaled_factor, flat, (((0,), (0,)), ((), ())), preferred_element_type=jnp.float32
    )
    core = product.astype(jnp.bfloat16).reshape(columns, data.shape[1], data.shape[2])
    return (core, factor)


def solution(mesh):
    in_specs = (P(None, "gx", "gy"), P(), P(), P())
    out_specs = (P(None, "gx", "gy"), P())
    return jax.shard_map(body, mesh=mesh, in_specs=in_specs, out_specs=out_specs, check_vma=False)
```

profile of v0, /device:TPU:1, one launch (start us, length us, event | category | flops | bytes accessed | tf_op | source)
XLA Modules:
  0.0 185.7 jit_solution(14243155040835074727)
XLA Ops:
  7.2 8.8 %fusion.7 = f32[128,128]{1,0:T(8,128)} fusion(bf16[128,128,128]{2,1,0:T(8,128)(2,1)} %param.7), kind=kOutput, calls=%fused_computation.6 | convolution fusion | flops 536870912 | bytes 4259840 | tf_op jit(solution)/shard_map/dot_general | solution.py:13
  16.7 122.8 %all-reduce.2.cloned.1.call-done = f32[128,128]{1,0:T(8,128)} async-done(((f32[128,128]{1,0:T(8,128)}), f32[128,128]{1,0:T(8,128)}) %all-reduce.2.cloned.1.call-update) | async-done | bytes 65552 | tf_op jit(solution)/shard_map/psum | solution.py:16
  139.5 1.1 fusion.14
  140.6 0.2 fusion.42
  140.9 2.9 %cholesky.74 = f32[32,32]{1,0:T(8,128)S(1)} custom-call(f32[32,32]{1,0:T(8,128)S(1)} %fusion.34), custom_call_target="Cholesky" | custom-call | tf_op jit(solution)/shard_map/jit(cholesky)/cholesky | solution.py:22
  143.9 0.6 compare_reduce_fusion.3
  144.5 0.7 fusion.23
  145.2 2.4 %custom-call.8 = f32[1,32,32]{1,2,0:T(8,128)S(1)} custom-call(f32[1,32,32]{2,1,0:T(8,128)S(1)} %fusion.23), custom_call_target="InvertDiagBlocksLowerTriangular" | custom-call | tf_op jit(solution)/shard_map/triangular_solve/custom-call.0 | solution.py:23
  147.6 0.2 convolution_bitcast_fusion.3
  147.8 1.1 fusion.13
  148.9 0.2 fusion.43
  149.2 2.9 %cholesky.85 = f32[32,32]{1,0:T(8,128)S(1)} custom-call(f32[32,32]{1,0:T(8,128)S(1)} %fusion.32), custom_call_target="Cholesky" | custom-call | tf_op jit(solution)/shard_map/jit(cholesky)/cholesky | solution.py:22
  152.2 0.6 compare_reduce_fusion.2
  152.8 0.7 fusion.24
  153.5 2.4 %custom-call.9 = f32[1,32,32]{1,2,0:T(8,128)S(1)} custom-call(f32[1,32,32]{2,1,0:T(8,128)S(1)} %fusion.24), custom_call_target="InvertDiagBlocksLowerTriangular" | custom-call | tf_op jit(solution)/shard_map/triangular_solve/custom-call.0 | solution.py:23
  155.9 0.2 convolution_bitcast_fusion.2
  156.1 1.1 fusion.12
  157.3 0.2 fusion.44
  157.5 2.9 %cholesky.96 = f32[32,32]{1,0:T(8,128)S(1)} custom-call(f32[32,32]{1,0:T(8,128)S(1)} %fusion.30), custom_call_target="Cholesky" | custom-call | tf_op jit(solution)/shard_map/jit(cholesky)/cholesky | solution.py:22
  160.5 0.6 compare_reduce_fusion.1
  161.1 0.7 fusion.25
  161.8 2.4 %custom-call.10 = f32[1,32,32]{1,2,0:T(8,128)S(1)} custom-call(f32[1,32,32]{2,1,0:T(8,128)S(1)} %fusion.25), custom_call_target="InvertDiagBlocksLowerTriangular" | custom-call | tf_op jit(solution)/shard_map/triangular_solve/custom-call.0 | solution.py:23
  164.2 0.2 convolution_bitcast_fusion.1
  164.5 1.1 fusion.11
  165.6 0.2 fusion.45
  165.8 2.9 %cholesky.107 = f32[32,32]{1,0:T(8,128)S(1)} custom-call(f32[32,32]{1,0:T(8,128)S(1)} %fusion.28), custom_call_target="Cholesky" | custom-call | tf_op jit(solution)/shard_map/jit(cholesky)/cholesky | solution.py:22
  168.8 0.6 compare_reduce_fusion
  169.4 0.7 fusion.26
  170.1 2.4 %custom-call.11 = f32[1,32,32]{1,2,0:T(8,128)S(1)} custom-call(f32[1,32,32]{2,1,0:T(8,128)S(1)} %fusion.26), custom_call_target="InvertDiagBlocksLowerTriangular" | custom-call | tf_op jit(solution)/shard_map/triangular_solve/custom-call.0 | solution.py:23
  172.5 0.2 fusion.10
  172.8 4.8 %fusion.4 = bf16[4,8,128,128]{3,1,2,0:T(8,128)(2,1)S(1)} fusion(bf16[16,8,128,128]{3,2,1,0:T(8,128)(2,1)} %bitcast.75, f32[128,32]{0,1:T(8,128)S(1)} %fusion.10, f32[128]{0:T(128)S(1)} %copy-done.1), kind=kOutput, calls=%fused_computation.5 | convolution fusion | flops 134750208 | bytes 5259776 | tf_op jit(solution)/shard_map/dot_general | solution.py:29
  177.6 1.2 copy.13
  (21 shorter events, 0.5 us)
Async XLA Ops:
  7.2 132.4 %copy-start = (f32[128,32]{0,1:T(8,128)S(1)}, f32[128,32]{0,1:T(8,128)}, u32[]{:S(2)}) copy-start(f32[128,32]{0,1:T(8,128)} %param.9) | copy-start | bytes 49156
  7.2 132.3 %copy-start.1 = (f32[128]{0:T(128)S(1)}, f32[128]{0:T(128)}, u32[]{:S(2)}) copy-start(f32[128]{0:T(128)} %param.8) | copy-start | bytes 1540
  7.2 132.3 %all-reduce.2.cloned.1.call-start = ((), (), s32[]{:S(2)}) async-start(), calls=%async_computation | async-start | bytes 131072 | tf_op jit(solution)/shard_map/psum | solution.py:16
  172.8 6.0 %copy-start.2 = (f32[128,32]{0,1:T(8,128)}, f32[128,32]{0,1:T(8,128)S(1)}, u32[]{:S(2)}) copy-start(f32[128,32]{0,1:T(8,128)S(1)} %fusion.10) | copy-start | bytes 49156
Sparse Core Ops, SparseCore 0:
  16.1 123.3 all-reduce.1
where the time goes:
time: 186 us
  waiting for transfers between devices  123 us (66%)
  other arithmetic  26.8 us (14%)
  matrix products  19.6 us (11%)
  between operations  14.9 us (8%)
    psum x1, waiting for transfers between devices, body(): gram = lax.psum(local_gram, ('gx', 'gy'))  123 us
    another operation x12, other arithmetic, body(): lower = jnp.linalg.cholesky(inner)  14.4 us
    another operation x8, other arithmetic, body(): lax.linalg.triangular_solve(lower, image, left_side=False, lower=True, tr...  12.3 us
    dot_general x1, matrix products, body(): lax.dot_general(flat, flat, (((1,), (1,)), ((), ())), preferred_element_t...  8.76 us
    dot_general x1, matrix products, body(): lax.dot_general(scaled_factor, flat, (((0,), (0,)), ((), ())), preferred_...  4.81 us
    dot_general x4, matrix products, body(): image = jnp.dot(weighted, basis, precision=lax.Precision.HIGHEST)  4.42 us
  transfers between devices with their start and end apart: 1, of which 1 were waited for; matrix products, arithmetic and copies ran while one was open for 0% of the time, Pallas kernels for 0%

commit v1 on v0

--- a/solution.py
+++ b/solution.py
@@ -13,7 +13,7 @@
     local_gram = lax.dot_general(
         flat, flat, (((1,), (1,)), ((), ())), preferred_element_type=jnp.float32
     )
-    gram = lax.psum(local_gram, ("gx", "gy"))
+    gram = lax.all_gather(local_gram, axis_name=("gx", "gy")).sum(axis=0)
     weighted = inv_scale[:, None] * gram * inv_scale[None, :]
     basis = start
     for turn in range(ITERS):

time: 186 us -> 120 us (0.65)
  waiting for transfers between devices: 123 us -> 58.2 us
  matrix products: 19.6 us -> 16.2 us
    psum x1 -> x0, waiting for transfers between devices: 123 us -> none  [body(): gram = lax.psum(local_gram, ('gx', 'gy'))]
    all_gather x0 -> x1, waiting for transfers between devices: none -> 58.1 us  [body(): gram = lax.all_gather(local_gram, axis_name=('gx', 'gy')).sum(axis=0)]
    dot_general x4, matrix products: 4.42 us -> 1.06 us  [body(): image = jnp.dot(weighted, basis, precision=lax.Precision.HIGHEST)]
where the time goes in v1:
time: 120 us; the launch traced here: 119 us
  waiting for transfers between devices  58.2 us (48%)
  other arithmetic  28.5 us (24%)
  matrix products  16.2 us (14%)
  between operations  14.9 us (12%)
  local copies, waits for them, and re-layouts  1.51 us (1%)
    all_gather x1, waiting for transfers between devices, body(): gram = lax.all_gather(local_gram, axis_name=('gx', 'gy')).sum(axis=0)  58.1 us
    another operation x12, other arithmetic, body(): lower = jnp.linalg.cholesky(inner)  14.4 us
    another operation x8, other arithmetic, body(): lax.linalg.triangular_solve(lower, image, left_side=False, lower=True, tr...  12.3 us
    dot_general x1, matrix products, body(): lax.dot_general(flat, flat, (((1,), (1,)), ((), ())), preferred_element_t...  8.76 us
    dot_general x1, matrix products, body(): lax.dot_general(scaled_factor, flat, (((0,), (0,)), ((), ())), preferred_...  4.81 us
  transfers between devices with their start and end apart: 1, of which 1 were waited for; matrix products, arithmetic and copies ran while one was open for 0% of the time, Pallas kernels for 0%

profile of v1, /device:TPU:1, one launch (start us, length us, event | category | flops | bytes accessed | tf_op | source)
XLA Modules:
  0.0 119.3 jit_solution(12483709167873759517)
XLA Ops:
  7.2 8.8 %fusion.7 = f32[128,128]{1,0:T(8,128)} fusion(bf16[128,128,128]{2,1,0:T(8,128)(2,1)} %param.7), kind=kOutput, calls=%fused_computation.6 | convolution fusion | flops 536870912 | bytes 4259840 | tf_op jit(solution)/shard_map/dot_general | solution.py:13
  16.7 58.1 %all-gather.3.cloned.1.call-done = f32[4096,128]{1,0:T(8,128)} async-done(((f32[128,128]{1,0:T(8,128)}), f32[4096,128]{1,0:T(8,128)}) %all-gather.3.cloned.1.call-update) | async-done | bytes 2097168 | tf_op jit(solution)/shard_map/all_gather | solution.py:16
  74.8 1.7 %reduce_sum.9 = f32[128,128]{1,0:T(8,128)S(1)} reduce(f32[32,128,128]{2,1,0:T(8,128)} %bitcast.77, f32[]{:T(128)} %constant.30.clone.1), dimensions={0}, to_apply=%region_0.0 | reduce | flops 507904 | bytes 2162692 | tf_op jit(solution)/shard_map/reduce_sum | solution.py:16
  76.5 0.3 fusion.14
  76.8 0.2 fusion.42
  77.1 2.9 %cholesky.74 = f32[32,32]{1,0:T(8,128)S(1)} custom-call(f32[32,32]{1,0:T(8,128)S(1)} %fusion.34), custom_call_target="Cholesky" | custom-call | tf_op jit(solution)/shard_map/jit(cholesky)/cholesky | solution.py:22
  80.0 0.6 compare_reduce_fusion.3
  80.7 0.7 fusion.23
  81.3 2.4 %custom-call.8 = f32[1,32,32]{1,2,0:T(8,128)S(1)} custom-call(f32[1,32,32]{2,1,0:T(8,128)S(1)} %fusion.23), custom_call_target="InvertDiagBlocksLowerTriangular" | custom-call | tf_op jit(solution)/shard_map/triangular_solve/custom-call.0 | solution.py:23
  83.8 0.2 convolution_bitcast_fusion.3
  84.0 0.3 fusion.13
  84.3 0.2 fusion.43
  84.6 2.9 %cholesky.85 = f32[32,32]{1,0:T(8,128)S(1)} custom-call(f32[32,32]{1,0:T(8,128)S(1)} %fusion.32), custom_call_target="Cholesky" | custom-call | tf_op jit(solution)/shard_map/jit(cholesky)/cholesky | solution.py:22
  87.5 0.6 compare_reduce_fusion.2
  88.2 0.7 fusion.24
  88.8 2.4 %custom-call.9 = f32[1,32,32]{1,2,0:T(8,128)S(1)} custom-call(f32[1,32,32]{2,1,0:T(8,128)S(1)} %fusion.24), custom_call_target="InvertDiagBlocksLowerTriangular" | custom-call | tf_op jit(solution)/shard_map/triangular_solve/custom-call.0 | solution.py:23
  91.3 0.2 convolution_bitcast_fusion.2
  91.5 0.3 fusion.12
  91.8 0.2 fusion.44
  92.0 2.9 %cholesky.96 = f32[32,32]{1,0:T(8,128)S(1)} custom-call(f32[32,32]{1,0:T(8,128)S(1)} %fusion.30), custom_call_target="Cholesky" | custom-call | tf_op jit(solution)/shard_map/jit(cholesky)/cholesky | solution.py:22
  95.0 0.6 compare_reduce_fusion.1
  95.6 0.7 fusion.25
  96.3 2.4 %custom-call.10 = f32[1,32,32]{1,2,0:T(8,128)S(1)} custom-call(f32[1,32,32]{2,1,0:T(8,128)S(1)} %fusion.25), custom_call_target="InvertDiagBlocksLowerTriangular" | custom-call | tf_op jit(solution)/shard_map/triangular_solve/custom-call.0 | solution.py:23
  98.7 0.2 convolution_bitcast_fusion.1
  99.0 0.3 fusion.11
  99.5 2.9 %cholesky.107 = f32[32,32]{1,0:T(8,128)S(1)} custom-call(f32[32,32]{1,0:T(8,128)S(1)} %fusion.28), custom_call_target="Cholesky" | custom-call | tf_op jit(solution)/shard_map/jit(cholesky)/cholesky | solution.py:22
  102.5 0.6 compare_reduce_fusion
  103.1 0.7 fusion.26
  103.8 2.4 %custom-call.11 = f32[1,32,32]{1,2,0:T(8,128)S(1)} custom-call(f32[1,32,32]{2,1,0:T(8,128)S(1)} %fusion.26), custom_call_target="InvertDiagBlocksLowerTriangular" | custom-call | tf_op jit(solution)/shard_map/triangular_solve/custom-call.0 | solution.py:23
  106.2 0.2 fusion.10
  106.5 4.8 %fusion.4 = bf16[4,8,128,128]{3,1,2,0:T(8,128)(2,1)S(1)} fusion(bf16[16,8,128,128]{3,2,1,0:T(8,128)(2,1)} %bitcast.76, f32[128,32]{0,1:T(8,128)S(1)} %fusion.10, f32[128]{0:T(128)S(1)} %copy-done.1), kind=kOutput, calls=%fused_computation.5 | convolution fusion | flops 134750208 | bytes 5259776 | tf_op jit(solution)/shard_map/dot_general | solution.py:29
  111.3 1.2 %copy.13 = bf16[4,8,128,128]{3,2,1,0:T(8,128)(2,1)} copy(bf16[4,8,128,128]{3,1,2,0:T(8,128)(2,1)S(1)} %fusion.4) | data formatting | bytes 2097152
  (22 shorter events, 0.7 us)
Async XLA Ops:
  7.2 69.4 %copy-start = (f32[128,32]{0,1:T(8,128)S(1)}, f32[128,32]{0,1:T(8,128)}, u32[]{:S(2)}) copy-start(f32[128,32]{0,1:T(8,128)} %param.9) | copy-start | bytes 49156
  7.2 69.4 %copy-start.1 = (f32[128]{0:T(128)S(1)}, f32[128]{0:T(128)}, u32[]{:S(2)}) copy-start(f32[128]{0:T(128)} %param.8) | copy-start | bytes 1540
  7.2 67.6 %all-gather.3.cloned.1.call-start = ((), (), s32[]{:S(2)}) async-start(), calls=%async_computation | async-start | bytes 2162688 | tf_op jit(solution)/shard_map/all_gather | solution.py:16
  106.4 6.0 %copy-start.2 = (f32[128,32]{0,1:T(8,128)}, f32[128,32]{0,1:T(8,128)S(1)}, u32[]{:S(2)}) copy-start(f32[128,32]{0,1:T(8,128)S(1)} %fusion.10) | copy-start | bytes 49156
Sparse Core Ops, SparseCore 0:
  16.1 58.6 all-gather.2
